TPU v7x, 256 devices: a whole 4x4x8 slice. The times are simulated.
256 devices in a mesh: sub: 64 (over x, z, core), blk: 4 (over y).
Axes of the slice: x: 4, y: 4, z: 8, core: 2. Of those that a mesh axis runs over, the one named last changes fastest.
Arguments:
- residual: float32 [64, 8, 375, 256], P('sub', 'blk'), may hold values from -6 to 6
- stiffness: bfloat16 [64, 8, 16, 375, 375], P('sub', 'blk'), may hold values from -0.078125 to 0.078125
- pattern: int32 [64, 8, 16], P('sub', 'blk'), may hold values from 0 to 7
- neumann_inv: bfloat16 [64, 8, 375, 375], P('sub', 'blk'), may hold values from -0.3125 to 0.3125
- dirichlet_inv: bfloat16 [64, 8, 375, 375], P('sub', 'blk'), may hold values from -0.3125 to 0.3125
- basis: bfloat16 [64, 8, 375, 192], P('sub', 'blk'), may hold values from -0.5 to 0.5
- node_ops: float32 [64, 6, 192, 192], P('sub'), as said below
- root_inv: float32 [192, 192], replicated, may hold values from -0.4375 to 0.4375
Outputs:
- preconditioned: float32 [64, 8, 375, 256], P('sub', 'blk')
Inputs may be any that keep to these rules, and one draw needn't show every extreme that they name: node_ops[s, l] equals node_ops[t, l] whenever s // 2**l == t // 2**l: one map for each tree node, held by all of its subdomains.
All inputs are finite; a program needn't handle non-finite values.
Results may differ from a plain program's by a relative error of at most 0.004.
Values may be sent and summed in bfloat16 or wider, within the bound.
A program may use at most 64 MiB of HBM per device.

v0:
```python
import jax
import jax.numpy as jnp
from jax import lax
from jax.sharding import PartitionSpec as P


def swapped(x, axis, distance):
    return lax.ppermute(x, axis, [(i, i ^ 1 << distance) for i in range(lax.axis_size(axis))])


def passed_along(x, axis, by):
    count = lax.axis_size(axis)
    pairs = [(i, i + by) for i in range(count) if 0 <= i + by < count]
    return lax.ppermute(x, axis, pairs)


def tree_solve(values, maps, root_inv):
    highest = lax.Precision.HIGHEST
    level_values = [values]
    current = values
    for level in range(maps.shape[0]):
        own = jnp.einsum("mk,mr->kr", maps[level], current, precision=highest)
        current = own + swapped(own, "sub", level)
        level_values.append(current)
    field = jnp.dot(root_inv, current, precision=highest)
    for level in reversed(range(maps.shape[0])):
        field = jnp.dot(maps[level], field, precision=highest) + level_values[level]
    return field


def shards(residual, stiffness, pattern, neumann_inv, dirichlet_inv, basis, node_ops, root_inv):
    subs = lax.axis_size("sub")
    here = lax.axis_index("sub")
    per_device = residual.shape[1]
    local_ids = jnp.arange(per_device)
    shared = (local_ids == 0) & (here > 0) | (local_ids == per_device - 1) & (here < subs - 1)
    scale = jnp.where(shared, 0.5, 1.0).astype(jnp.float32)[:, None, None]
    scaled_bf = (residual[0] * scale).astype(jnp.bfloat16)
    local_fix = jnp.einsum(
        "jab,jbr->jar", neumann_inv[0], scaled_bf, preferred_element_type=jnp.float32
    )
    partial_coarse = jnp.einsum(
        "jbm,jbr->mr", basis[0], scaled_bf, preferred_element_type=jnp.float32
    )
    total = lax.psum(partial_coarse, "blk")
    coarse_fix = tree_solve(total, node_ops[0], root_inv).astype(jnp.bfloat16)
    fix_term = jnp.einsum("jbm,mr->jbr", basis[0], coarse_fix, preferred_element_type=jnp.float32)
    combined = ((local_fix + fix_term) * scale)[None]
    incoming = passed_along(combined[:, -1], "sub", 1)
    first = combined[:, 0] + incoming
    returned = passed_along(first, "sub", -1)
    last = jnp.where(here < subs - 1, returned, combined[:, -1])
    assembled = jnp.concatenate([first[:, None], combined[:, 1:-1], last[:, None]], axis=1)
    assembled_bf = assembled.astype(jnp.bfloat16)
    gathered = lax.all_gather(assembled_bf, "blk", axis=1, tiled=True)
    picked = jnp.take(gathered[0], pattern[0], axis=0)
    coupled = jnp.einsum("jpab,jpbr->jar", stiffness[0], picked, preferred_element_type=jnp.float32)
    correction = jnp.einsum(
        "jab,jbr->jar",
        dirichlet_inv[0],
        coupled.astype(jnp.bfloat16),
        preferred_element_type=jnp.float32,
    )
    result = assembled[0] - jnp.where(shared[:, None, None], 0.0, correction)
    return result[None]


def solution(mesh):
    placed = (
        P("sub", "blk", None, None),
        P("sub", "blk", None, None, None),
        P("sub", "blk", None),
        P("sub", "blk", None, None),
        P("sub", "blk", None, None),
        P("sub", "blk", None, None),
        P("sub", None, None, None),
        P(),
    )
    return jax.shard_map(
        shards, mesh=mesh, in_specs=placed, out_specs=P("sub", "blk", None, None), check_vma=False
    )
```

profile of v0, /device:TPU:1, one launch (start us, length us, event | category | flops | bytes accessed | tf_op | source)
XLA Modules:
  0.0 188.2 jit_solution(13424925944676565091)
XLA Ops:
  6.6 2.3 %convolution_bitcast_fusion.14 = f32[192,256]{1,0:T(8,128)} fusion(bf16[1,2,375,192]{2,3,1,0:T(8,128)(2,1)} %param.13, f32[1,2,375,256]{3,1,2,0:T(2,128)} %param.8, f32[2]{0:T(128)S(1)} %get-tuple-element.5), kind=kOutput, calls=%fused_computation.31 | convolution fusion | flops 74112000 | bytes 1252616 | tf_op jit(solution)/shard_map/jbm,jbr->mr/dot_general | solution.py:42
  8.9 0.0 all-reduce.2.cloned.1.call-update
  8.9 0.0 all-gather.2.cloned.1.call-start
  8.9 49.2 %all-reduce.2.cloned.1.call-done = f32[192,256]{1,0:T(8,128)} async-done(((f32[192,256]{1,0:T(8,128)}), f32[192,256]{1,0:T(8,128)}) %all-reduce.2.cloned.1.call-update) | async-done | bytes 196624 | tf_op jit(solution)/shard_map/psum | solution.py:45
  58.2 1.5 convolution_bitcast_fusion.13
  59.7 2.9 %collective-permute-start = (f32[192,256]{1,0:T(8,128)S(1)}, f32[192,256]{1,0:T(8,128)S(1)}, u32[]{:S(2)}, u32[]{:S(2)}) collective-permute-start(f32[192,256]{1,0:T(8,128)S(1)} %convolution_bitcast_fusion.13), channel_id=1, source_target_pairs={{0,4},{4,0},{8,12},{12,8},{16,20},{20,16},{24,28},{28,24},{32,36},... | collective-permute-start | bytes 589832 | tf_op jit(solution)/shard_map/ppermute | solution.py:8
  62.6 1.1 collective-permute-done
  63.6 0.6 convolution_bitcast_fusion.12
  64.2 1.4 collective-permute-start.1
  65.6 4.8 %collective-permute-done.1 = f32[192,256]{1,0:T(8,128)S(1)} collective-permute-done((f32[192,256]{1,0:T(8,128)S(1)}, f32[192,256]{1,0:T(8,128)S(1)}, u32[]{:S(2)}, u32[]{:S(2)}) %collective-permute-start.1) | collective-permute-done | bytes 196640 | tf_op jit(solution)/shard_map/ppermute | solution.py:8
  70.4 0.6 convolution_bitcast_fusion.11
  71.0 2.3 %collective-permute-start.2 = (f32[192,256]{1,0:T(8,128)S(1)}, f32[192,256]{1,0:T(8,128)S(1)}, u32[]{:S(2)}, u32[]{:S(2)}) collective-permute-start(f32[192,256]{1,0:T(8,128)S(1)} %convolution_bitcast_fusion.11), channel_id=1, source_target_pairs={{0,16},{4,20},{8,24},{12,28},{16,0},{20,4},{24,8},{28,12},{32,48},... | collective-permute-start | bytes 589832 | tf_op jit(solution)/shard_map/ppermute | solution.py:8
  73.4 8.7 %collective-permute-done.2 = f32[192,256]{1,0:T(8,128)S(1)} collective-permute-done((f32[192,256]{1,0:T(8,128)S(1)}, f32[192,256]{1,0:T(8,128)S(1)}, u32[]{:S(2)}, u32[]{:S(2)}) %collective-permute-start.2) | collective-permute-done | bytes 196640 | tf_op jit(solution)/shard_map/ppermute | solution.py:8
  82.1 0.6 convolution_bitcast_fusion.10
  82.7 6.4 %collective-permute-start.3 = (f32[192,256]{1,0:T(8,128)S(1)}, f32[192,256]{1,0:T(8,128)S(1)}, u32[]{:S(2)}, u32[]{:S(2)}) collective-permute-start(f32[192,256]{1,0:T(8,128)S(1)} %convolution_bitcast_fusion.10), channel_id=1, source_target_pairs={{0,32},{4,36},{8,40},{12,44},{16,48},{20,52},{24,56},{28,60},{32,0... | collective-permute-start | bytes 589832 | tf_op jit(solution)/shard_map/ppermute | solution.py:8
  89.1 7.4 %collective-permute-done.3 = f32[192,256]{1,0:T(8,128)S(1)} collective-permute-done((f32[192,256]{1,0:T(8,128)S(1)}, f32[192,256]{1,0:T(8,128)S(1)}, u32[]{:S(2)}, u32[]{:S(2)}) %collective-permute-start.3) | collective-permute-done | bytes 196640 | tf_op jit(solution)/shard_map/ppermute | solution.py:8
  96.6 0.6 convolution_bitcast_fusion.9
  97.2 1.3 collective-permute-start.4
  98.4 3.9 %collective-permute-done.4 = f32[192,256]{1,0:T(8,128)S(1)} collective-permute-done((f32[192,256]{1,0:T(8,128)S(1)}, f32[192,256]{1,0:T(8,128)S(1)}, u32[]{:S(2)}, u32[]{:S(2)}) %collective-permute-start.4) | collective-permute-done | bytes 196640 | tf_op jit(solution)/shard_map/ppermute | solution.py:8
  102.3 0.6 convolution_bitcast_fusion.8
  102.9 2.8 %collective-permute-start.5 = (f32[192,256]{1,0:T(8,128)S(1)}, f32[192,256]{1,0:T(8,128)S(1)}, u32[]{:S(2)}, u32[]{:S(2)}) collective-permute-start(f32[192,256]{1,0:T(8,128)S(1)} %convolution_bitcast_fusion.8), channel_id=1, source_target_pairs={{0,128},{4,132},{8,136},{12,140},{16,144},{20,148},{24,152},{28,15... | collective-permute-start | bytes 589832 | tf_op jit(solution)/shard_map/ppermute | solution.py:8
  105.7 3.3 %collective-permute-done.5 = f32[192,256]{1,0:T(8,128)S(1)} collective-permute-done((f32[192,256]{1,0:T(8,128)S(1)}, f32[192,256]{1,0:T(8,128)S(1)}, u32[]{:S(2)}, u32[]{:S(2)}) %collective-permute-start.5) | collective-permute-done | bytes 196640 | tf_op jit(solution)/shard_map/ppermute | solution.py:8
  109.0 0.3 fusion.52
  109.4 0.3 fusion.23
  109.7 0.3 fusion.22
  110.0 0.3 fusion.21
  110.4 0.3 fusion.20
  110.7 0.3 fusion.19
  111.1 0.3 fusion.25
  111.4 0.3 convolution_bitcast_fusion.1
  111.8 0.1 copy-done.2
  111.9 0.4 fusion.12
  112.3 0.1 fusion.70
  112.4 0.4 copy.61
  112.8 2.7 %collective-permute-start.6 = (f32[1,375,256]{2,0,1:T(1,128)S(1)}, f32[1,375,256]{2,0,1:T(1,128)S(1)}, u32[]{:S(2)}, u32[]{:S(2)}) collective-permute-start(f32[1,375,256]{2,0,1:T(1,128)S(1)} %bitcast.158), channel_id=1, source_target_pairs={{0,4},{4,8},{8,12},{12,16},{16,20},{20,24},{24,28},{28,32},{32,36}... | collective-permute-start | bytes 1152008 | tf_op jit(solution)/shard_map/ppermute | solution.py:14
  115.5 4.6 %collective-permute-done.6 = f32[1,375,256]{2,0,1:T(1,128)S(1)} collective-permute-done((f32[1,375,256]{2,0,1:T(1,128)S(1)}, f32[1,375,256]{2,0,1:T(1,128)S(1)}, u32[]{:S(2)}, u32[]{:S(2)}) %collective-permute-start.6) | collective-permute-done | bytes 384032 | tf_op jit(solution)/shard_map/ppermute | solution.py:14
  120.1 0.5 fusion.36
  120.6 2.1 %collective-permute-start.7 = (f32[1,375,256]{2,0,1:T(1,128)S(1)}, f32[1,375,256]{2,0,1:T(1,128)S(1)}, u32[]{:S(2)}, u32[]{:S(2)}) collective-permute-start(f32[1,375,256]{2,0,1:T(1,128)S(1)} %fusion.36), channel_id=1, source_target_pairs={{4,0},{8,4},{12,8},{16,12},{20,16},{24,20},{28,24},{32,28},{36,32}... | collective-permute-start | bytes 1152008 | tf_op jit(solution)/shard_map/ppermute | solution.py:14
  122.7 7.6 %collective-permute-done.7 = f32[1,375,256]{2,0,1:T(1,128)S(1)} collective-permute-done((f32[1,375,256]{2,0,1:T(1,128)S(1)}, f32[1,375,256]{2,0,1:T(1,128)S(1)}, u32[]{:S(2)}, u32[]{:S(2)}) %collective-permute-start.7) | collective-permute-done | bytes 384032 | tf_op jit(solution)/shard_map/ppermute | solution.py:14
  130.3 0.5 fusion.35
  130.8 0.7 fusion.39
  131.6 0.8 copy.30
  132.3 0.0 all-gather.2.cloned.1.call-update
  132.4 0.1 reshape.96
  132.5 31.0 %all-gather.2.cloned.1.call-done = bf16[1,8,375,256]{3,2,0,1:T(8,128)(2,1)} async-done(((bf16[1,2,375,256]{3,2,0,1:T(8,128)(2,1)}), bf16[1,8,375,256]{3,2,0,1:T(8,128)(2,1)}) %all-gather.2.cloned.1.call-update) | async-done | bytes 1536016 | tf_op jit(solution)/shard_map/all_gather | solution.py:55
  163.5 5.0 %gather_fusion = bf16[32,375,256]{2,1,0:T(8,128)(2,1)} fusion(bf16[8,375,256]{2,1,0:T(8,128)(2,1)} %bitcast.154, s32[1024]{0:T(1024)S(1)} %pad_clamp_fusion), kind=kCustom, calls=%fused_computation | custom fusion | bytes 12288128 | tf_op jit(solution)/shard_map/jit(_take)/gather | solution.py:56
  168.5 11.0 %fusion.28 = f32[2,256,375]{1,2,0:T(8,128)S(1)} fusion(bf16[2,375,375]{2,0,1:T(2,128)(2,1)S(1)} %bitcast.160, bf16[2,16,375,375]{3,1,2,0:T(8,128)(2,1)} %bitcast.159, bf16[2,16,375,256]{3,2,1,0:T(8,128)(2,1)} %bitcast.155, pred[2,16]{1,0:T(4,128)(4,1)S(1)} %compare_and_fusion), kind=kOutput, calls=%fused_computation.41 | convolution fusion | flops 2451264000 | bytes 16474532 | tf_op jit(solution)/shard_map/jab,jbr->jar/dot_general | solution.py:58
  179.6 1.8 fusion.27
  (25 shorter events, 0.2 us)
Async XLA Ops:
  6.5 105.2 %copy-start = (bf16[1,2,375,375]{3,1,2,0:T(2,128)(2,1)S(1)}, bf16[1,2,375,375]{3,1,2,0:T(2,128)(2,1)}, u32[]{:S(2)}) copy-start(bf16[1,2,375,375]{3,1,2,0:T(2,128)(2,1)} %param.11) | copy-start | bytes 1687504
  6.5 51.6 %copy-start.1 = (f32[1,6,192,192]{3,2,1,0:T(8,128)S(1)}, f32[1,6,192,192]{3,2,1,0:T(8,128)}, u32[]{:S(2)}) copy-start(f32[1,6,192,192]{3,2,1,0:T(8,128)} %param.14) | copy-start | bytes 2654212
  6.5 51.6 %all-reduce.2.cloned.1.call-start = ((), (), s32[]{:S(2)}) async-start(), calls=%async_computation | async-start | bytes 393216 | tf_op jit(solution)/shard_map/psum | solution.py:45
  8.9 154.6 %all-gather.2.cloned.1.call-start = ((), (), s32[]{:S(2)}) async-start(), calls=%async_computation.1 | async-start | bytes 1925120 | tf_op jit(solution)/shard_map/all_gather | solution.py:55
  59.7 3.9 %collective-permute-start = (f32[192,256]{1,0:T(8,128)S(1)}, f32[192,256]{1,0:T(8,128)S(1)}, u32[]{:S(2)}, u32[]{:S(2)}) collective-permute-start(f32[192,256]{1,0:T(8,128)S(1)} %convolution_bitcast_fusion.13), channel_id=1, source_target_pairs={{0,4},{4,0},{8,12},{12,8},{16,20},{20,16},{24,28},{28,24},{32,36},... | collective-permute-start | bytes 589832 | tf_op jit(solution)/shard_map/ppermute | solution.py:8
  64.2 6.2 %collective-permute-start.1 = (f32[192,256]{1,0:T(8,128)S(1)}, f32[192,256]{1,0:T(8,128)S(1)}, u32[]{:S(2)}, u32[]{:S(2)}) collective-permute-start(f32[192,256]{1,0:T(8,128)S(1)} %convolution_bitcast_fusion.12), channel_id=1, source_target_pairs={{0,8},{4,12},{8,0},{12,4},{16,24},{20,28},{24,16},{28,20},{32,40},... | collective-permute-start | bytes 589832 | tf_op jit(solution)/shard_map/ppermute | solution.py:8
  71.0 11.0 %collective-permute-start.2 = (f32[192,256]{1,0:T(8,128)S(1)}, f32[192,256]{1,0:T(8,128)S(1)}, u32[]{:S(2)}, u32[]{:S(2)}) collective-permute-start(f32[192,256]{1,0:T(8,128)S(1)} %convolution_bitcast_fusion.11), channel_id=1, source_target_pairs={{0,16},{4,20},{8,24},{12,28},{16,0},{20,4},{24,8},{28,12},{32,48},... | collective-permute-start | bytes 589832 | tf_op jit(solution)/shard_map/ppermute | solution.py:8
  82.7 26.4 %copy-start.5 = (f32[192,192]{1,0:T(8,128)S(1)}, f32[192,192]{1,0:T(8,128)}, u32[]{:S(2)}) copy-start(f32[192,192]{1,0:T(8,128)} %param.15) | copy-start | bytes 442372
  82.7 13.9 %collective-permute-start.3 = (f32[192,256]{1,0:T(8,128)S(1)}, f32[192,256]{1,0:T(8,128)S(1)}, u32[]{:S(2)}, u32[]{:S(2)}) collective-permute-start(f32[192,256]{1,0:T(8,128)S(1)} %convolution_bitcast_fusion.10), channel_id=1, source_target_pairs={{0,32},{4,36},{8,40},{12,44},{16,48},{20,52},{24,56},{28,60},{32,0... | collective-permute-start | bytes 589832 | tf_op jit(solution)/shard_map/ppermute | solution.py:8
  97.2 5.1 %collective-permute-start.4 = (f32[192,256]{1,0:T(8,128)S(1)}, f32[192,256]{1,0:T(8,128)S(1)}, u32[]{:S(2)}, u32[]{:S(2)}) collective-permute-start(f32[192,256]{1,0:T(8,128)S(1)} %convolution_bitcast_fusion.9), channel_id=1, source_target_pairs={{0,64},{4,68},{8,72},{12,76},{16,80},{20,84},{24,88},{28,92},{32,9... | collective-permute-start | bytes 589832 | tf_op jit(solution)/shard_map/ppermute | solution.py:8
  102.9 6.1 %collective-permute-start.5 = (f32[192,256]{1,0:T(8,128)S(1)}, f32[192,256]{1,0:T(8,128)S(1)}, u32[]{:S(2)}, u32[]{:S(2)}) collective-permute-start(f32[192,256]{1,0:T(8,128)S(1)} %convolution_bitcast_fusion.8), channel_id=1, source_target_pairs={{0,128},{4,132},{8,136},{12,140},{16,144},{20,148},{24,152},{28,15... | collective-permute-start | bytes 589832 | tf_op jit(solution)/shard_map/ppermute | solution.py:8
  110.0 1.0 copy-start.4
  110.4 1.0 copy-start.3
  110.7 1.1 copy-start.2
  112.8 7.3 %collective-permute-start.6 = (f32[1,375,256]{2,0,1:T(1,128)S(1)}, f32[1,375,256]{2,0,1:T(1,128)S(1)}, u32[]{:S(2)}, u32[]{:S(2)}) collective-permute-start(f32[1,375,256]{2,0,1:T(1,128)S(1)} %bitcast.158), channel_id=1, source_target_pairs={{0,4},{4,8},{8,12},{12,16},{16,20},{20,24},{24,28},{28,32},{32,36}... | collective-permute-start | bytes 1152008 | tf_op jit(solution)/shard_map/ppermute | solution.py:14
  120.6 9.7 %collective-permute-start.7 = (f32[1,375,256]{2,0,1:T(1,128)S(1)}, f32[1,375,256]{2,0,1:T(1,128)S(1)}, u32[]{:S(2)}, u32[]{:S(2)}) collective-permute-start(f32[1,375,256]{2,0,1:T(1,128)S(1)} %fusion.36), channel_id=1, source_target_pairs={{4,0},{8,4},{12,8},{16,12},{20,16},{24,20},{28,24},{32,28},{36,32}... | collective-permute-start | bytes 1152008 | tf_op jit(solution)/shard_map/ppermute | solution.py:14
  130.8 1.5 copy-start.6
  163.5 5.0 %copy-start.7 = (bf16[1,2,375,375]{3,1,2,0:T(2,128)(2,1)S(1)}, bf16[1,2,375,375]{3,1,2,0:T(2,128)(2,1)}, u32[]{:S(2)}) copy-start(bf16[1,2,375,375]{3,1,2,0:T(2,128)(2,1)} %param.12) | copy-start | bytes 1687504
Sparse Core Ops, SparseCore 0:
  9.7 48.4 all-reduce.1
  132.5 30.9 all-gather.1
where the time goes:
time: 188 us
  waiting for transfers between devices  122 us (65%)
  starting transfers between devices  21.9 us (12%)
  matrix products  20.8 us (11%)
  between operations  13.6 us (7%)
  local copies, waits for them, and re-layouts  6.44 us (3%)
  other arithmetic  3.71 us (2%)
    psum x1, waiting for transfers between devices, shards(): total = lax.psum(partial_coarse, 'blk')  49.2 us
    all_gather x1, waiting for transfers between devices, shards(): gathered = lax.all_gather(assembled_bf, 'blk', axis=1, tiled=True)  31 us
    ppermute x6, waiting for transfers between devices, swapped(): lax.ppermute(x, axis, [(i, i ^ 1 << distance) for i in range(lax.axis_siz...  29.2 us
    ppermute x6, starting transfers between devices, swapped(): lax.ppermute(x, axis, [(i, i ^ 1 << distance) for i in range(lax.axis_siz...  17.1 us
    ppermute x2, waiting for transfers between devices, passed_along(): return lax.ppermute(x, axis, pairs)  12.2 us
    dot_general x1, matrix products, shards(): jnp.einsum('jab,jbr->jar', dirichlet_inv[0], coupled.astype(jnp.bfloat16)...  11 us
    gather x1, local copies, waits for them, and re-layouts, shards(): picked = jnp.take(gathered[0], pattern[0], axis=0)  5.01 us
    ppermute x2, starting transfers between devices, passed_along(): return lax.ppermute(x, axis, pairs)  4.79 us
  transfers between devices with their start and end apart: 10, of which 10 were waited for; matrix products, arithmetic and copies ran while one was open for 0% of the time, Pallas kernels for 0%

commit v1 on v0

--- a/solution.py
+++ b/solution.py
@@ -2,6 +2,7 @@
 import jax.numpy as jnp
 from jax import lax
 from jax.sharding import PartitionSpec as P
+from jax.lax import all_gather
 
 
 def swapped(x, axis, distance):
@@ -42,7 +43,7 @@
     partial_coarse = jnp.einsum(
         "jbm,jbr->mr", basis[0], scaled_bf, preferred_element_type=jnp.float32
     )
-    total = lax.psum(partial_coarse, "blk")
+    total = jnp.sum(all_gather(partial_coarse, "blk"), axis=0)
     coarse_fix = tree_solve(total, node_ops[0], root_inv).astype(jnp.bfloat16)
     fix_term = jnp.einsum("jbm,mr->jbr", basis[0], coarse_fix, preferred_element_type=jnp.float32)
     combined = ((local_fix + fix_term) * scale)[None]

time: 188 us -> 153 us (0.81)
  waiting for transfers between devices: 122 us -> 81.9 us
  blocking collectives: 0 us -> 13.3 us
  starting transfers between devices: 21.9 us -> 14.7 us
    psum x1 -> x0, waiting for transfers between devices: 49.2 us -> none  [shards(): total = lax.psum(partial_coarse, 'blk')]
    all_gather x0 -> x1, blocking collectives: none -> 13.3 us  [shards(): total = jnp.sum(all_gather(partial_coarse, 'blk'), axis=0)]
    ppermute x6, waiting for transfers between devices: 29.2 us -> 38.2 us  [swapped(): lax.ppermute(x, axis, [(i, i ^ 1 << distance) for i in range(lax.axis_siz...]
    ppermute x6, starting transfers between devices: 17.1 us -> 10.6 us  [swapped(): lax.ppermute(x, axis, [(i, i ^ 1 << distance) for i in range(lax.axis_siz...]
  transfers between devices with their start and end apart: 10 -> 9, of which waited for: 10 -> 9; matrix products, arithmetic and copies ran while one was open for 0% -> 0% of each run, Pallas kernels for 0% -> 0%
where the time goes in v1:
time: 153 us
  waiting for transfers between devices  81.9 us (54%)
  matrix products  19.1 us (12%)
  starting transfers between devices  14.7 us (10%)
  between operations  13.7 us (9%)
  blocking collectives  13.3 us (9%)
  local copies, waits for them, and re-layouts  6.47 us (4%)
  other arithmetic  3.76 us (2%)
    ppermute x6, waiting for transfers between devices, swapped(): lax.ppermute(x, axis, [(i, i ^ 1 << distance) for i in range(lax.axis_siz...  38.2 us
    all_gather x1, waiting for transfers between devices, shards(): gathered = lax.all_gather(assembled_bf, 'blk', axis=1, tiled=True)  31.5 us
    all_gather x1, blocking collectives, shards(): total = jnp.sum(all_gather(partial_coarse, 'blk'), axis=0)  13.3 us
    ppermute x2, waiting for transfers between devices, passed_along(): return lax.ppermute(x, axis, pairs)  12.2 us
    dot_general x1, matrix products, shards(): jnp.einsum('jab,jbr->jar', dirichlet_inv[0], coupled.astype(jnp.bfloat16)...  11 us
    ppermute x6, starting transfers between devices, swapped(): lax.ppermute(x, axis, [(i, i ^ 1 << distance) for i in range(lax.axis_siz...  10.6 us
    gather x1, local copies, waits for them, and re-layouts, shards(): picked = jnp.take(gathered[0], pattern[0], axis=0)  5.03 us
    ppermute x2, starting transfers between devices, passed_along(): return lax.ppermute(x, axis, pairs)  4.02 us
  transfers between devices with their start and end apart: 9, of which 9 were waited for; matrix products, arithmetic and copies ran while one was open for 0% of the time, Pallas kernels for 0%

profile of v1, /device:TPU:1, one launch (start us, length us, event | category | flops | bytes accessed | tf_op | source)
XLA Modules:
  0.0 153.0 jit_solution(7815360209997608733)
XLA Ops:
  6.5 1.6 %convolution_bitcast_fusion.14 = f32[192,256]{1,0:T(8,128)S(1)} fusion(bf16[1,2,375,192]{2,3,1,0:T(8,128)(2,1)} %param.13, f32[1,2,375,256]{3,1,2,0:T(2,128)} %param.8, f32[2]{0:T(128)S(1)} %get-tuple-element.5), kind=kOutput, calls=%fused_computation.31 | convolution fusion | flops 74112000 | bytes 1252616 | tf_op jit(solution)/shard_map/jbm,jbr->mr/dot_general | solution.py:43
  8.1 13.3 %all-gather = f32[768,256]{1,0:T(8,128)S(1)} all-gather(f32[192,256]{1,0:T(8,128)S(1)} %convolution_bitcast_fusion.14), channel_id=2, replica_groups=mesh['sub'=64,'blk'=4] {'blk'}, dimensions={0}, use_global_device_ids=true | all-gather | bytes 983040 | tf_op jit(solution)/shard_map/all_gather | solution.py:46
  21.5 0.1 reduce_sum.9
  21.5 0.6 convolution_bitcast_fusion.13
  22.1 4.2 %collective-permute-start = (f32[192,256]{1,0:T(8,128)S(1)}, f32[192,256]{1,0:T(8,128)S(1)}, u32[]{:S(2)}, u32[]{:S(2)}) collective-permute-start(f32[192,256]{1,0:T(8,128)S(1)} %convolution_bitcast_fusion.13), channel_id=1, source_target_pairs={{0,4},{4,0},{8,12},{12,8},{16,20},{20,16},{24,28},{28,24},{32,36},... | collective-permute-start | bytes 589832 | tf_op jit(solution)/shard_map/ppermute | solution.py:9
  26.3 1.1 collective-permute-done
  27.4 0.6 convolution_bitcast_fusion.12
  28.0 0.1 collective-permute-start.1
  28.1 6.1 %collective-permute-done.1 = f32[192,256]{1,0:T(8,128)S(1)} collective-permute-done((f32[192,256]{1,0:T(8,128)S(1)}, f32[192,256]{1,0:T(8,128)S(1)}, u32[]{:S(2)}, u32[]{:S(2)}) %collective-permute-start.1) | collective-permute-done | bytes 196640 | tf_op jit(solution)/shard_map/ppermute | solution.py:9
  34.2 0.6 convolution_bitcast_fusion.11
  34.8 1.4 collective-permute-start.2
  36.2 10.6 %collective-permute-done.2 = f32[192,256]{1,0:T(8,128)S(1)} collective-permute-done((f32[192,256]{1,0:T(8,128)S(1)}, f32[192,256]{1,0:T(8,128)S(1)}, u32[]{:S(2)}, u32[]{:S(2)}) %collective-permute-start.2) | collective-permute-done | bytes 196640 | tf_op jit(solution)/shard_map/ppermute | solution.py:9
  46.8 0.6 convolution_bitcast_fusion.10
  47.4 4.6 %collective-permute-start.3 = (f32[192,256]{1,0:T(8,128)S(1)}, f32[192,256]{1,0:T(8,128)S(1)}, u32[]{:S(2)}, u32[]{:S(2)}) collective-permute-start(f32[192,256]{1,0:T(8,128)S(1)} %convolution_bitcast_fusion.10), channel_id=1, source_target_pairs={{0,32},{4,36},{8,40},{12,44},{16,48},{20,52},{24,56},{28,60},{32,0... | collective-permute-start | bytes 589832 | tf_op jit(solution)/shard_map/ppermute | solution.py:9
  52.0 9.6 %collective-permute-done.3 = f32[192,256]{1,0:T(8,128)S(1)} collective-permute-done((f32[192,256]{1,0:T(8,128)S(1)}, f32[192,256]{1,0:T(8,128)S(1)}, u32[]{:S(2)}, u32[]{:S(2)}) %collective-permute-start.3) | collective-permute-done | bytes 196640 | tf_op jit(solution)/shard_map/ppermute | solution.py:9
  61.6 0.6 convolution_bitcast_fusion.9
  62.2 0.1 collective-permute-start.4
  62.3 5.0 %collective-permute-done.4 = f32[192,256]{1,0:T(8,128)S(1)} collective-permute-done((f32[192,256]{1,0:T(8,128)S(1)}, f32[192,256]{1,0:T(8,128)S(1)}, u32[]{:S(2)}, u32[]{:S(2)}) %collective-permute-start.4) | collective-permute-done | bytes 196640 | tf_op jit(solution)/shard_map/ppermute | solution.py:9
  67.4 0.6 convolution_bitcast_fusion.8
  68.0 0.3 collective-permute-start.5
  68.2 5.8 %collective-permute-done.5 = f32[192,256]{1,0:T(8,128)S(1)} collective-permute-done((f32[192,256]{1,0:T(8,128)S(1)}, f32[192,256]{1,0:T(8,128)S(1)}, u32[]{:S(2)}, u32[]{:S(2)}) %collective-permute-start.5) | collective-permute-done | bytes 196640 | tf_op jit(solution)/shard_map/ppermute | solution.py:9
  74.1 0.3 fusion.52
  74.4 0.3 fusion.23
  74.7 0.3 fusion.22
  75.1 0.3 fusion.21
  75.4 0.0 copy-start.3
  75.4 0.3 fusion.20
  75.8 0.3 fusion.19
  76.1 0.3 fusion.25
  76.5 0.3 convolution_bitcast_fusion.1
  76.8 0.1 copy-done.2
  76.9 0.4 fusion.12
  77.3 0.1 fusion.70
  77.4 0.4 copy.61
  77.8 1.9 %collective-permute-start.6 = (f32[1,375,256]{2,0,1:T(1,128)S(1)}, f32[1,375,256]{2,0,1:T(1,128)S(1)}, u32[]{:S(2)}, u32[]{:S(2)}) collective-permute-start(f32[1,375,256]{2,0,1:T(1,128)S(1)} %bitcast.160), channel_id=1, source_target_pairs={{0,4},{4,8},{8,12},{12,16},{16,20},{20,24},{24,28},{28,32},{32,36}... | collective-permute-start | bytes 1152008 | tf_op jit(solution)/shard_map/ppermute | solution.py:15
  79.7 4.6 %collective-permute-done.6 = f32[1,375,256]{2,0,1:T(1,128)S(1)} collective-permute-done((f32[1,375,256]{2,0,1:T(1,128)S(1)}, f32[1,375,256]{2,0,1:T(1,128)S(1)}, u32[]{:S(2)}, u32[]{:S(2)}) %collective-permute-start.6) | collective-permute-done | bytes 384032 | tf_op jit(solution)/shard_map/ppermute | solution.py:15
  84.3 0.5 fusion.36
  84.9 2.1 %collective-permute-start.7 = (f32[1,375,256]{2,0,1:T(1,128)S(1)}, f32[1,375,256]{2,0,1:T(1,128)S(1)}, u32[]{:S(2)}, u32[]{:S(2)}) collective-permute-start(f32[1,375,256]{2,0,1:T(1,128)S(1)} %fusion.36), channel_id=1, source_target_pairs={{4,0},{8,4},{12,8},{16,12},{20,16},{24,20},{28,24},{32,28},{36,32}... | collective-permute-start | bytes 1152008 | tf_op jit(solution)/shard_map/ppermute | solution.py:15
  87.0 7.6 %collective-permute-done.7 = f32[1,375,256]{2,0,1:T(1,128)S(1)} collective-permute-done((f32[1,375,256]{2,0,1:T(1,128)S(1)}, f32[1,375,256]{2,0,1:T(1,128)S(1)}, u32[]{:S(2)}, u32[]{:S(2)}) %collective-permute-start.7) | collective-permute-done | bytes 384032 | tf_op jit(solution)/shard_map/ppermute | solution.py:15
  94.6 0.5 fusion.35
  95.1 0.7 fusion.39
  95.8 0.8 copy.30
  96.6 0.0 all-gather.3.cloned.1.call-update
  96.7 0.1 reshape.96
  96.8 31.5 %all-gather.3.cloned.1.call-done = bf16[1,8,375,256]{3,2,0,1:T(8,128)(2,1)} async-done(((bf16[1,2,375,256]{3,2,0,1:T(8,128)(2,1)}), bf16[1,8,375,256]{3,2,0,1:T(8,128)(2,1)}) %all-gather.3.cloned.1.call-update) | async-done | bytes 1536016 | tf_op jit(solution)/shard_map/all_gather | solution.py:56
  128.2 5.0 %gather_fusion = bf16[32,375,256]{2,1,0:T(8,128)(2,1)} fusion(bf16[8,375,256]{2,1,0:T(8,128)(2,1)} %bitcast.155, s32[1024]{0:T(1024)S(1)} %pad_clamp_fusion), kind=kCustom, calls=%fused_computation | custom fusion | bytes 12288128 | tf_op jit(solution)/shard_map/jit(_take)/gather | solution.py:57
  133.2 11.0 %fusion.28 = f32[2,256,375]{1,2,0:T(8,128)S(1)} fusion(bf16[2,375,375]{2,0,1:T(2,128)(2,1)S(1)} %bitcast.162, bf16[2,16,375,375]{3,1,2,0:T(8,128)(2,1)} %bitcast.161, bf16[2,16,375,256]{3,2,1,0:T(8,128)(2,1)} %bitcast.156, pred[2,16]{1,0:T(4,128)(4,1)S(1)} %compare_and_fusion), kind=kOutput, calls=%fused_computation.41 | convolution fusion | flops 2451264000 | bytes 16474532 | tf_op jit(solution)/shard_map/jab,jbr->jar/dot_general | solution.py:59
  144.3 1.8 %fusion.27 = f32[1,2,375,256]{3,1,2,0:T(2,128)} fusion(f32[2,256,375]{1,2,0:T(8,128)S(1)} %fusion.28, pred[2]{0:T(512)(128)(4,1)S(1)} %get-tuple-element.6, f32[1,1,375,256]{3,1,2,0:T(1,128)S(1)} %fusion.35, f32[1,1,375,256]{3,1,2,0:T(1,128)S(1)} %bitcast.158), kind=kLoop, calls=%fused_computation.38 | loop fusion | flops 576000 | bytes 2304002 | tf_op jit(solution)/shard_map/broadcast_in_dim | solution.py:66
  (22 shorter events, 0.2 us)
Async XLA Ops:
  6.5 70.3 %copy-start = (bf16[1,2,375,375]{3,1,2,0:T(2,128)(2,1)S(1)}, bf16[1,2,375,375]{3,1,2,0:T(2,128)(2,1)}, u32[]{:S(2)}) copy-start(bf16[1,2,375,375]{3,1,2,0:T(2,128)(2,1)} %param.11) | copy-start | bytes 1687504
  6.5 121.7 %all-gather.3.cloned.1.call-start = ((), (), s32[]{:S(2)}) async-start(), calls=%async_computation | async-start | bytes 1925120 | tf_op jit(solution)/shard_map/all_gather | solution.py:56
  8.1 13.4 %copy-start.1 = (f32[1,6,192,192]{3,2,1,0:T(8,128)S(1)}, f32[1,6,192,192]{3,2,1,0:T(8,128)}, u32[]{:S(2)}) copy-start(f32[1,6,192,192]{3,2,1,0:T(8,128)} %param.14) | copy-start | bytes 2654212
  22.1 5.3 %collective-permute-start = (f32[192,256]{1,0:T(8,128)S(1)}, f32[192,256]{1,0:T(8,128)S(1)}, u32[]{:S(2)}, u32[]{:S(2)}) collective-permute-start(f32[192,256]{1,0:T(8,128)S(1)} %convolution_bitcast_fusion.13), channel_id=1, source_target_pairs={{0,4},{4,0},{8,12},{12,8},{16,20},{20,16},{24,28},{28,24},{32,36},... | collective-permute-start | bytes 589832 | tf_op jit(solution)/shard_map/ppermute | solution.py:9
  28.0 6.2 %collective-permute-start.1 = (f32[192,256]{1,0:T(8,128)S(1)}, f32[192,256]{1,0:T(8,128)S(1)}, u32[]{:S(2)}, u32[]{:S(2)}) collective-permute-start(f32[192,256]{1,0:T(8,128)S(1)} %convolution_bitcast_fusion.12), channel_id=1, source_target_pairs={{0,8},{4,12},{8,0},{12,4},{16,24},{20,28},{24,16},{28,20},{32,40},... | collective-permute-start | bytes 589832 | tf_op jit(solution)/shard_map/ppermute | solution.py:9
  34.8 12.0 %collective-permute-start.2 = (f32[192,256]{1,0:T(8,128)S(1)}, f32[192,256]{1,0:T(8,128)S(1)}, u32[]{:S(2)}, u32[]{:S(2)}) collective-permute-start(f32[192,256]{1,0:T(8,128)S(1)} %convolution_bitcast_fusion.11), channel_id=1, source_target_pairs={{0,16},{4,20},{8,24},{12,28},{16,0},{20,4},{24,8},{28,12},{32,48},... | collective-permute-start | bytes 589832 | tf_op jit(solution)/shard_map/ppermute | solution.py:9
  47.4 26.6 %copy-start.4 = (f32[192,192]{1,0:T(8,128)S(1)}, f32[192,192]{1,0:T(8,128)}, u32[]{:S(2)}) copy-start(f32[192,192]{1,0:T(8,128)} %param.15) | copy-start | bytes 442372
  47.4 14.2 %collective-permute-start.3 = (f32[192,256]{1,0:T(8,128)S(1)}, f32[192,256]{1,0:T(8,128)S(1)}, u32[]{:S(2)}, u32[]{:S(2)}) collective-permute-start(f32[192,256]{1,0:T(8,128)S(1)} %convolution_bitcast_fusion.10), channel_id=1, source_target_pairs={{0,32},{4,36},{8,40},{12,44},{16,48},{20,52},{24,56},{28,60},{32,0... | collective-permute-start | bytes 589832 | tf_op jit(solution)/shard_map/ppermute | solution.py:9
  62.2 5.1 %collective-permute-start.4 = (f32[192,256]{1,0:T(8,128)S(1)}, f32[192,256]{1,0:T(8,128)S(1)}, u32[]{:S(2)}, u32[]{:S(2)}) collective-permute-start(f32[192,256]{1,0:T(8,128)S(1)} %convolution_bitcast_fusion.9), channel_id=1, source_target_pairs={{0,64},{4,68},{8,72},{12,76},{16,80},{20,84},{24,88},{28,92},{32,9... | collective-permute-start | bytes 589832 | tf_op jit(solution)/shard_map/ppermute | solution.py:9
  68.0 6.1 %collective-permute-start.5 = (f32[192,256]{1,0:T(8,128)S(1)}, f32[192,256]{1,0:T(8,128)S(1)}, u32[]{:S(2)}, u32[]{:S(2)}) collective-permute-start(f32[192,256]{1,0:T(8,128)S(1)} %convolution_bitcast_fusion.8), channel_id=1, source_target_pairs={{0,128},{4,132},{8,136},{12,140},{16,144},{20,148},{24,152},{28,15... | collective-permute-start | bytes 589832 | tf_op jit(solution)/shard_map/ppermute | solution.py:9
  75.4 1.0 copy-start.3
  75.8 1.1 copy-start.2
  77.8 6.5 %collective-permute-start.6 = (f32[1,375,256]{2,0,1:T(1,128)S(1)}, f32[1,375,256]{2,0,1:T(1,128)S(1)}, u32[]{:S(2)}, u32[]{:S(2)}) collective-permute-start(f32[1,375,256]{2,0,1:T(1,128)S(1)} %bitcast.160), channel_id=1, source_target_pairs={{0,4},{4,8},{8,12},{12,16},{16,20},{20,24},{24,28},{28,32},{32,36}... | collective-permute-start | bytes 1152008 | tf_op jit(solution)/shard_map/ppermute | solution.py:15
  84.9 9.7 %collective-permute-start.7 = (f32[1,375,256]{2,0,1:T(1,128)S(1)}, f32[1,375,256]{2,0,1:T(1,128)S(1)}, u32[]{:S(2)}, u32[]{:S(2)}) collective-permute-start(f32[1,375,256]{2,0,1:T(1,128)S(1)} %fusion.36), channel_id=1, source_target_pairs={{4,0},{8,4},{12,8},{16,12},{20,16},{24,20},{28,24},{32,28},{36,32}... | collective-permute-start | bytes 1152008 | tf_op jit(solution)/shard_map/ppermute | solution.py:15
  95.1 1.5 copy-start.5
  128.2 5.0 %copy-start.6 = (bf16[1,2,375,375]{3,1,2,0:T(2,128)(2,1)S(1)}, bf16[1,2,375,375]{3,1,2,0:T(2,128)(2,1)}, u32[]{:S(2)}) copy-start(bf16[1,2,375,375]{3,1,2,0:T(2,128)(2,1)} %param.12) | copy-start | bytes 1687504
Sparse Core Ops, SparseCore 0:
  96.8 31.4 all-gather.2
